TPU v7x, 128 devices: a whole 4x4x4 slice. The times are simulated.
128 devices in a mesh: cam: 16 (over y, x), pts: 8 (over z, core).
Axes of the slice: x: 4, y: 4, z: 4, core: 2. Of those that a mesh axis runs over, the one named last changes fastest.
Arguments:
- rhs: float32 [9, 131072], P(None, 'cam'), may hold values from -6 to 6
- cam_block: float32 [9, 9, 131072], P(None, None, 'cam'), as said below
- coupling: bfloat16 [512, 144, 12288], P('pts', None, 'cam'), may hold values from -0.03125 to 0.03125
- point_inverse: float32 [3, 3, 32768], P(None, None, 'pts'), as said below
- precond: float32 [9, 9, 131072], P(None, None, 'cam'), as said below
- tile_index: int32 [512, 64], P('pts', 'cam'), may hold values from 0 to 511
- tile_count: int32 [512, 16], P('pts', 'cam'), may hold values from 1 to 4, as said below
Outputs:
- solution: float32 [9, 131072], P(None, 'cam')
- residual: float32 [9, 131072], P(None, 'cam')
Inputs may be any that keep to these rules, and one draw needn't show every extreme that they name: `tile_count`: every entry is at least 1 and at most 4; both ends occur. `cam_block`: symmetric with a dominant positive diagonal for each camera. `precond`: symmetric with a dominant positive diagonal for each camera. `point_inverse`: symmetric with a dominant positive diagonal for each point.
All inputs are finite; a program needn't handle non-finite values.
Results may differ from a plain program's by a relative error of at most 0.0024.
Values may be sent and summed in bfloat16 or wider, within the bound.
A program may use at most 128 MiB of HBM per device.

v0:
```python
import jax
import jax.numpy as jnp
from jax import lax
from jax.sharding import PartitionSpec as P

ITERS = 3


def camera_tiles(vector):
    comps, count = vector.shape
    return (
        vector.reshape(comps, count // 16, 16).transpose(1, 0, 2).reshape(count // 16, comps * 16)
    )


def camera_cols(tiles):
    count = tiles.shape[0]
    return tiles.reshape(count, 9, 16).transpose(1, 0, 2).reshape(9, count * 16)


def point_cols(tiles):
    count = tiles.shape[0]
    return tiles.reshape(count, 3, 64).transpose(1, 0, 2).reshape(3, count * 64)


def point_tiles(vector):
    count = vector.shape[1] // 64
    return vector.reshape(3, count, 64).transpose(1, 0, 2).reshape(count, 192)


def per_device(rhs, cam_block, coupling, point_inverse, precond, tile_index, tile_count):
    tiles_here, slot_count = tile_index.shape
    cam_count = rhs.shape[1] // 16
    blocks = coupling.reshape(tiles_here, 144, slot_count, 192)
    usable = (jnp.arange(slot_count)[None, :] < tile_count).astype(jnp.bfloat16)
    flat_index = tile_index.reshape(-1)
    onehot_t = (jnp.arange(cam_count)[:, None] == flat_index[None, :]).astype(
        jnp.float32
    ) * usable.reshape(1, -1).astype(jnp.float32)

    def global_sum(value):
        return lax.psum(value, "cam")

    solution = jnp.zeros_like(rhs)
    residual = rhs
    precond_res = jnp.sum(precond * residual[None, :, :], axis=1)
    direction = precond_res
    inner_now = global_sum(jnp.sum(residual * precond_res))
    for iteration in range(ITERS):
        dir_rows = jnp.take(
            camera_tiles(direction.astype(jnp.bfloat16)), flat_index, axis=0
        ).reshape(tiles_here, slot_count, 144)
        dir_rows = dir_rows * usable[:, :, None]
        point_part = jnp.einsum(
            "tckp,tkc->tp", blocks, dir_rows, preferred_element_type=jnp.float32
        )
        point_part = point_cols(point_part)
        summed = lax.psum(point_part.astype(jnp.bfloat16), "cam").astype(jnp.float32)
        solved = jnp.sum(point_inverse * summed[None, :, :], axis=1).astype(jnp.bfloat16)
        contrib = jnp.einsum(
            "tckp,tp->tkc", blocks, point_tiles(solved), preferred_element_type=jnp.float32
        )
        cam_part = jnp.dot(
            onehot_t,
            contrib.reshape(-1, 144),
            precision=lax.Precision.HIGHEST,
            preferred_element_type=jnp.float32,
        )
        image = jnp.sum(cam_block * direction[None, :, :], axis=1) - lax.psum(
            camera_cols(cam_part).astype(jnp.bfloat16), "pts"
        ).astype(jnp.float32)
        step_size = inner_now / global_sum(jnp.sum(direction * image))
        solution = solution + step_size * direction
        residual = residual - step_size * image
        if iteration + 1 < ITERS:
            precond_res = jnp.sum(precond * residual[None, :, :], axis=1)
            inner_new = global_sum(jnp.sum(residual * precond_res))
            direction = precond_res + inner_new / inner_now * direction
            inner_now = inner_new
    return (solution, residual)


def solution(mesh):
    in_specs = (
        P(None, "cam"),
        P(None, None, "cam"),
        P("pts", None, "cam"),
        P(None, None, "pts"),
        P(None, None, "cam"),
        P("pts", "cam"),
        P("pts", "cam"),
    )
    out_specs = (P(None, "cam"), P(None, "cam"))
    return jax.shard_map(
        per_device, mesh=mesh, in_specs=in_specs, out_specs=out_specs, check_vma=False
    )
```

profile of v0, /device:TPU:0, one launch (start us, length us, event | category | flops | bytes accessed | tf_op | source)
XLA Modules:
  0.0 773.3 jit_solution(13054918832175976593)
XLA Ops:
  7.2 0.8 copy.25
  8.1 3.4 multiply_reduce_fusion.5
  11.6 1.1 convert_element_type.149
  13.2 1.2 gather_fusion
  14.6 35.9 %reshape.168 = bf16[64,144,4,192]{3,2,1,0:T(4,128)(2,1)} reshape(bf16[64,144,768]{2,1,0:T(8,128)(2,1)} %param.11) | data formatting | bytes 28311552 | tf_op jit(solution)/shard_map/reshape | solution.py:34
  50.6 9.1 %fusion.7 = bf16[64,1,192,1]{2,1,3,0:T(2,128)(2,1)S(1)} fusion(bf16[64,144,4,192]{3,2,1,0:T(4,128)(2,1)} %reshape.168, bf16[64,4,144,1]{2,1,0,3:T(4,128)(2,1)S(1)} %multiply_bitcast_fusion.2), kind=kOutput, calls=%fused_computation.13 | convolution fusion | flops 14155776 | bytes 14254080 | tf_op jit(solution)/shard_map/tckp,tkc->tp/dot_general | solution.py:54
  60.1 75.1 %psum.85 = bf16[3,4096]{1,0:T(4,128)(2,1)S(1)} all-reduce(bf16[3,4096]{1,0:T(4,128)(2,1)S(1)} %convert_element_type.154), channel_id=1, replica_groups=mesh['cam'=16,'pts'=8] {'cam'}, use_global_device_ids=true, to_apply=%region_4.6 | all-reduce | flops 12288 | bytes 49152 | tf_op jit(solution)/shard_map/psum | solution.py:58
  135.7 16.4 %fusion = f32[64,144,4]{2,1,0:T(8,128)} fusion(f32[64,192]{1,0:T(8,128)S(1)} %copy.66, bf16[64,144,4,192]{3,2,1,0:T(4,128)(2,1)} %reshape.168), kind=kLoop, calls=%fused_computation.6 | loop fusion | flops 21196800 | bytes 14352384
  152.1 4.1 copy.51
  156.5 0.8 fusion.9
  157.8 2.5 convert_element_type.160
  160.4 3.3 multiply_reduce_fusion.4
  163.7 54.2 %all-reduce.5.cloned.1.call-done = bf16[9,8192]{1,0:T(8,128)(2,1)} async-done(((bf16[9,8192]{1,0:T(8,128)(2,1)}), bf16[9,8192]{1,0:T(8,128)(2,1)}) %all-reduce.5.cloned.1.call-update) | async-done | bytes 147472 | tf_op jit(solution)/shard_map/psum | solution.py:69
  217.9 1.7 multiply_reduce_fusion.10
  219.6 40.9 %all-reduce = (f32[]{:T(128)}, f32[]{:T(128)}) all-reduce(f32[]{:T(128)} %get-tuple-element.4, f32[]{:T(128)} %get-tuple-element.3), channel_id=1, replica_groups=mesh['cam'=16,'pts'=8] {'cam'}, use_global_device_ids=true, to_apply=%region_2.0 | all-reduce | flops 2 | bytes 16 | tf_op jit(solution)/shard_map/psum | solution.py:42
  261.8 1.0 multiply_subtract_fusion.2
  262.9 3.3 multiply_reduce_fusion.3
  266.9 36.6 %psum.88 = f32[]{:T(128)} all-reduce(f32[]{:T(128)} %multiply_reduce_fusion.9), channel_id=1, replica_groups=mesh['cam'=16,'pts'=8] {'cam'}, use_global_device_ids=true, to_apply=%region_11.13 | all-reduce | flops 1 | bytes 8 | tf_op jit(solution)/shard_map/psum | solution.py:42
  304.8 1.1 convert_element_type.163
  306.4 1.2 gather_fusion.1
  307.9 9.1 %fusion.5 = bf16[64,1,192,1]{2,1,3,0:T(2,128)(2,1)S(1)} fusion(bf16[64,144,4,192]{3,2,1,0:T(4,128)(2,1)} %reshape.168, bf16[64,4,144,1]{2,1,0,3:T(4,128)(2,1)S(1)} %multiply_bitcast_fusion.1), kind=kOutput, calls=%fused_computation.11 | convolution fusion | flops 14155776 | bytes 14254080 | tf_op jit(solution)/shard_map/tckp,tkc->tp/dot_general | solution.py:54
  317.3 71.4 %psum.89 = bf16[3,4096]{1,0:T(4,128)(2,1)S(1)} all-reduce(bf16[3,4096]{1,0:T(4,128)(2,1)S(1)} %convert_element_type.167), channel_id=1, replica_groups=mesh['cam'=16,'pts'=8] {'cam'}, use_global_device_ids=true, to_apply=%region_13.15 | all-reduce | flops 12288 | bytes 49152 | tf_op jit(solution)/shard_map/psum | solution.py:58
  389.2 16.4 %fusion.1 = f32[64,144,4]{2,1,0:T(8,128)} fusion(f32[64,192]{1,0:T(8,128)S(1)} %copy.67, bf16[64,144,4,192]{3,2,1,0:T(4,128)(2,1)} %reshape.168), kind=kLoop, calls=%fused_computation.7 | loop fusion | flops 21196800 | bytes 14352384
  405.6 4.1 copy.58
  409.9 0.8 fusion.10
  411.2 2.5 convert_element_type.173
  413.8 3.3 multiply_reduce_fusion.2
  417.1 50.6 %all-reduce.7.cloned.1.call-done = bf16[9,8192]{1,0:T(8,128)(2,1)} async-done(((bf16[9,8192]{1,0:T(8,128)(2,1)}), bf16[9,8192]{1,0:T(8,128)(2,1)}) %all-reduce.7.cloned.1.call-update) | async-done | bytes 147472 | tf_op jit(solution)/shard_map/psum | solution.py:69
  467.7 1.7 multiply_reduce_fusion.8
  469.4 41.1 %psum.91 = f32[]{:T(128)} all-reduce(f32[]{:T(128)} %multiply_reduce_fusion.8), channel_id=1, replica_groups=mesh['cam'=16,'pts'=8] {'cam'}, use_global_device_ids=true, to_apply=%region_17.19 | all-reduce | flops 1 | bytes 8 | tf_op jit(solution)/shard_map/psum | solution.py:42
  511.7 1.0 multiply_subtract_fusion.1
  512.8 3.3 multiply_reduce_fusion.1
  516.8 36.1 %psum.92 = f32[]{:T(128)} all-reduce(f32[]{:T(128)} %multiply_reduce_fusion.7), channel_id=1, replica_groups=mesh['cam'=16,'pts'=8] {'cam'}, use_global_device_ids=true, to_apply=%region_20.22 | all-reduce | flops 1 | bytes 8 | tf_op jit(solution)/shard_map/psum | solution.py:42
  554.1 0.8 fusion.35
  554.9 1.9 add.63
  556.9 1.0 copy.38
  557.9 1.0 copy.39
  558.9 1.2 gather_fusion.2
  560.4 9.1 %fusion.3 = bf16[64,1,192,1]{2,1,3,0:T(2,128)(2,1)S(1)} fusion(bf16[64,144,4,192]{3,2,1,0:T(4,128)(2,1)} %reshape.168, bf16[64,4,144,1]{2,1,0,3:T(4,128)(2,1)S(1)} %multiply_bitcast_fusion), kind=kOutput, calls=%fused_computation.9 | convolution fusion | flops 14155776 | bytes 14254080 | tf_op jit(solution)/shard_map/tckp,tkc->tp/dot_general | solution.py:54
  569.8 71.7 %psum.93 = bf16[3,4096]{1,0:T(4,128)(2,1)S(1)} all-reduce(bf16[3,4096]{1,0:T(4,128)(2,1)S(1)} %convert_element_type.178), channel_id=1, replica_groups=mesh['cam'=16,'pts'=8] {'cam'}, use_global_device_ids=true, to_apply=%region_22.24 | all-reduce | flops 12288 | bytes 49152 | tf_op jit(solution)/shard_map/psum | solution.py:58
  642.1 16.4 %fusion.2 = f32[64,144,4]{2,1,0:T(8,128)} fusion(f32[64,192]{1,0:T(8,128)S(1)} %copy.68, bf16[64,144,4,192]{3,2,1,0:T(4,128)(2,1)} %reshape.168), kind=kLoop, calls=%fused_computation.8 | loop fusion | flops 21196800 | bytes 14352384
  658.4 4.1 copy.65
  664.0 2.5 convert_element_type.184
  666.6 3.3 multiply_reduce_fusion
  669.9 50.6 %all-reduce.9.cloned.1.call-done = bf16[9,8192]{1,0:T(8,128)(2,1)} async-done(((bf16[9,8192]{1,0:T(8,128)(2,1)}), bf16[9,8192]{1,0:T(8,128)(2,1)}) %all-reduce.9.cloned.1.call-update) | async-done | bytes 147472 | tf_op jit(solution)/shard_map/psum | solution.py:69
  720.5 1.7 multiply_reduce_fusion.6
  722.2 40.9 %psum.95 = f32[]{:T(128)} all-reduce(f32[]{:T(128)} %multiply_reduce_fusion.6), channel_id=1, replica_groups=mesh['cam'=16,'pts'=8] {'cam'}, use_global_device_ids=true, to_apply=%region_26.28 | all-reduce | flops 1 | bytes 8 | tf_op jit(solution)/shard_map/psum | solution.py:42
  764.5 2.1 multiply_subtract_fusion
  (72 shorter events, 9.2 us)
Async XLA Ops:
  7.2 210.7 %all-reduce.5.cloned.1.call-start = ((), (), s32[]{:S(2)}) async-start(), calls=%async_computation | async-start | bytes 524288 | tf_op jit(solution)/shard_map/psum | solution.py:69
  8.1 6.4 copy-start.2
  50.6 84.6 %copy-start.1 = (f32[3,3,4096]{2,1,0:T(4,128)S(1)}, f32[3,3,4096]{2,1,0:T(4,128)}, u32[]{:S(2)}) copy-start(f32[3,3,4096]{2,1,0:T(4,128)} %param.12) | copy-start | bytes 442372
  156.4 61.4 %copy-start = (f32[9,8192]{1,0:T(8,128)S(1)}, f32[9,8192]{1,0:T(8,128)}, u32[]{:S(2)}) copy-start(f32[9,8192]{1,0:T(8,128)} %param.9) | copy-start | bytes 884740
  160.4 307.3 %all-reduce.7.cloned.1.call-start = ((), (), s32[]{:S(2)}) async-start(), calls=%async_computation.1 | async-start | bytes 524288 | tf_op jit(solution)/shard_map/psum | solution.py:69
  413.7 306.8 %all-reduce.9.cloned.1.call-start = ((), (), s32[]{:S(2)}) async-start(), calls=%async_computation.2 | async-start | bytes 524288 | tf_op jit(solution)/shard_map/psum | solution.py:69
Sparse Core Ops, SparseCore 0:
  160.5 57.3 all-reduce.4
  413.8 53.7 all-reduce.6
  666.7 53.7 all-reduce.8
where the time goes:
time: 781 us; the launch traced here: 773 us
  blocking collectives  414 us (53%)
  waiting for transfers between devices  155 us (20%)
  other arithmetic  82 us (10%)
  local copies, waits for them, and re-layouts  71.4 us (9%)
  matrix products  29.6 us (4%)
  between operations  20.8 us (3%)
    psum x3, blocking collectives, per_device(): lax.psum(point_part.astype(jnp.bfloat16), 'cam').astype(jnp.float32)  218 us
    psum x5, blocking collectives, global_sum(): return lax.psum(value, 'cam')  196 us
    psum x3, waiting for transfers between devices, per_device(): lax.psum(camera_cols(cam_part).astype(jnp.bfloat16), 'pts')  155 us
    unnamed x6, other arithmetic  49.2 us
    reshape x1, local copies, waits for them, and re-layouts, per_device(): blocks = coupling.reshape(tiles_here, 144, slot_count, 192)  35.9 us
    dot_general x3, matrix products, per_device(): jnp.einsum('tckp,tkc->tp', blocks, dir_rows, preferred_element_type=jnp.f...  27.4 us
  transfers between devices with their start and end apart: 3, of which 3 were waited for; matrix products, arithmetic and copies ran while one was open for 1% of the time, Pallas kernels for 0%

commit v1 on v0

--- a/solution.py
+++ b/solution.py
@@ -55,7 +55,9 @@
             "tckp,tkc->tp", blocks, dir_rows, preferred_element_type=jnp.float32
         )
         point_part = point_cols(point_part)
-        summed = lax.psum(point_part.astype(jnp.bfloat16), "cam").astype(jnp.float32)
+        summed = jnp.sum(lax.all_gather(point_part.astype(jnp.bfloat16), "cam"), axis=0).astype(
+            jnp.float32
+        )
         solved = jnp.sum(point_inverse * summed[None, :, :], axis=1).astype(jnp.bfloat16)
         contrib = jnp.einsum(
             "tckp,tp->tkc", blocks, point_tiles(solved), preferred_element_type=jnp.float32

time: 781 us -> 641 us (0.82)
  blocking collectives: 414 us -> 266 us
  waiting for transfers between devices: 155 us -> 163 us
    psum x3 -> x0, blocking collectives: 218 us -> none  [per_device(): lax.psum(point_part.astype(jnp.bfloat16), 'cam').astype(jnp.float32)]
    all_gather x0 -> x3, blocking collectives: none -> 70.6 us  [per_device(): lax.all_gather(point_part.astype(jnp.bfloat16), 'cam')]
    psum x3, waiting for transfers between devices: 155 us -> 163 us  [per_device(): lax.psum(camera_cols(cam_part).astype(jnp.bfloat16), 'pts')]
  transfers between devices with their start and end apart: 3 -> 3, of which waited for: 3 -> 3; matrix products, arithmetic and copies ran while one was open for 1% -> 2% of each run, Pallas kernels for 0% -> 0%
where the time goes in v1:
time: 641 us; the launch traced here: 634 us
  blocking collectives  266 us (41%)
  waiting for transfers between devices  163 us (25%)
  other arithmetic  82.6 us (13%)
  local copies, waits for them, and re-layouts  71.4 us (11%)
  matrix products  29.6 us (5%)
  between operations  20.9 us (3%)
    psum x5, blocking collectives, global_sum(): return lax.psum(value, 'cam')  196 us
    psum x3, waiting for transfers between devices, per_device(): lax.psum(camera_cols(cam_part).astype(jnp.bfloat16), 'pts')  163 us
    all_gather x3, blocking collectives, per_device(): lax.all_gather(point_part.astype(jnp.bfloat16), 'cam')  70.6 us
    unnamed x6, other arithmetic  49.2 us
    reshape x1, local copies, waits for them, and re-layouts, per_device(): blocks = coupling.reshape(tiles_here, 144, slot_count, 192)  35.9 us
    dot_general x3, matrix products, per_device(): jnp.einsum('tckp,tkc->tp', blocks, dir_rows, preferred_element_type=jnp.f...  27.4 us
  transfers between devices with their start and end apart: 3, of which 3 were waited for; matrix products, arithmetic and copies ran while one was open for 2% of the time, Pallas kernels for 0%

profile of v1, /device:TPU:0, one launch (start us, length us, event | category | flops | bytes accessed | tf_op | source)
XLA Modules:
  0.0 634.2 jit_solution(16441384432490718578)
XLA Ops:
  7.2 0.8 copy.47
  8.1 3.4 multiply_reduce_fusion.5
  11.6 1.1 convert_element_type.188
  13.2 1.2 gather_fusion
  14.6 35.9 %reshape.204 = bf16[64,144,4,192]{3,2,1,0:T(4,128)(2,1)} reshape(bf16[64,144,768]{2,1,0:T(8,128)(2,1)} %param.11) | data formatting | bytes 28311552 | tf_op jit(solution)/shard_map/reshape | solution.py:34
  50.6 9.1 %fusion.7 = bf16[64,1,192,1]{2,1,3,0:T(2,128)(2,1)S(1)} fusion(bf16[64,144,4,192]{3,2,1,0:T(4,128)(2,1)} %reshape.204, bf16[64,4,144,1]{2,1,0,3:T(4,128)(2,1)S(1)} %multiply_bitcast_fusion.2), kind=kOutput, calls=%fused_computation.13 | convolution fusion | flops 14155776 | bytes 14254080 | tf_op jit(solution)/shard_map/tckp,tkc->tp/dot_general | solution.py:54
  60.1 24.6 %all_gather.12 = bf16[16,3,4096]{2,1,0:T(4,128)(2,1)S(1)} all-gather(bf16[1,3,4096]{2,1,0:T(4,128)(2,1)S(1)} %convert_element_type.193), channel_id=1, replica_groups=mesh['cam'=16,'pts'=8] {'cam'}, dimensions={0}, use_global_device_ids=true | all-gather | bytes 417792 | tf_op jit(solution)/shard_map/all_gather | solution.py:58
  85.5 16.4 %fusion = f32[64,144,4]{2,1,0:T(8,128)} fusion(f32[64,192]{1,0:T(8,128)S(1)} %copy.88, bf16[64,144,4,192]{3,2,1,0:T(4,128)(2,1)} %reshape.204), kind=kLoop, calls=%fused_computation.6 | loop fusion | flops 21196800 | bytes 14352384
  101.9 4.1 copy.73
  106.3 0.8 fusion.9
  107.6 2.5 convert_element_type.199
  110.2 3.3 multiply_reduce_fusion.4
  113.5 57.1 %all-reduce.5.cloned.1.call-done = bf16[9,8192]{1,0:T(8,128)(2,1)} async-done(((bf16[9,8192]{1,0:T(8,128)(2,1)}), bf16[9,8192]{1,0:T(8,128)(2,1)}) %all-reduce.5.cloned.1.call-update) | async-done | bytes 147472 | tf_op jit(solution)/shard_map/psum | solution.py:71
  170.5 1.7 multiply_reduce_fusion.10
  172.2 40.9 %all-reduce = (f32[]{:T(128)}, f32[]{:T(128)}) all-reduce(f32[]{:T(128)} %get-tuple-element.4, f32[]{:T(128)} %get-tuple-element.3), channel_id=1, replica_groups=mesh['cam'=16,'pts'=8] {'cam'}, use_global_device_ids=true, to_apply=%region_2.0 | all-reduce | flops 2 | bytes 16 | tf_op jit(solution)/shard_map/psum | solution.py:42
  214.5 1.0 multiply_subtract_fusion.2
  215.5 3.3 multiply_reduce_fusion.3
  219.6 36.6 %psum.66 = f32[]{:T(128)} all-reduce(f32[]{:T(128)} %multiply_reduce_fusion.9), channel_id=1, replica_groups=mesh['cam'=16,'pts'=8] {'cam'}, use_global_device_ids=true, to_apply=%region_11.13 | all-reduce | flops 1 | bytes 8 | tf_op jit(solution)/shard_map/psum | solution.py:42
  257.5 1.1 convert_element_type.202
  259.1 1.2 gather_fusion.1
  260.5 9.1 %fusion.5 = bf16[64,1,192,1]{2,1,3,0:T(2,128)(2,1)S(1)} fusion(bf16[64,144,4,192]{3,2,1,0:T(4,128)(2,1)} %reshape.204, bf16[64,4,144,1]{2,1,0,3:T(4,128)(2,1)S(1)} %multiply_bitcast_fusion.1), kind=kOutput, calls=%fused_computation.11 | convolution fusion | flops 14155776 | bytes 14254080 | tf_op jit(solution)/shard_map/tckp,tkc->tp/dot_general | solution.py:54
  270.0 22.9 %all_gather.13 = bf16[16,3,4096]{2,1,0:T(4,128)(2,1)S(1)} all-gather(bf16[1,3,4096]{2,1,0:T(4,128)(2,1)S(1)} %convert_element_type.206), channel_id=1, replica_groups=mesh['cam'=16,'pts'=8] {'cam'}, dimensions={0}, use_global_device_ids=true | all-gather | bytes 417792 | tf_op jit(solution)/shard_map/all_gather | solution.py:58
  293.6 16.4 %fusion.1 = f32[64,144,4]{2,1,0:T(8,128)} fusion(f32[64,192]{1,0:T(8,128)S(1)} %copy.89, bf16[64,144,4,192]{3,2,1,0:T(4,128)(2,1)} %reshape.204), kind=kLoop, calls=%fused_computation.7 | loop fusion | flops 21196800 | bytes 14352384
  310.0 4.1 copy.80
  315.6 2.5 convert_element_type.212
  318.2 3.3 multiply_reduce_fusion.2
  321.5 53.1 %all-reduce.7.cloned.1.call-done = bf16[9,8192]{1,0:T(8,128)(2,1)} async-done(((bf16[9,8192]{1,0:T(8,128)(2,1)}), bf16[9,8192]{1,0:T(8,128)(2,1)}) %all-reduce.7.cloned.1.call-update) | async-done | bytes 147472 | tf_op jit(solution)/shard_map/psum | solution.py:71
  374.6 1.7 multiply_reduce_fusion.8
  376.2 41.1 %psum.68 = f32[]{:T(128)} all-reduce(f32[]{:T(128)} %multiply_reduce_fusion.8), channel_id=1, replica_groups=mesh['cam'=16,'pts'=8] {'cam'}, use_global_device_ids=true, to_apply=%region_17.19 | all-reduce | flops 1 | bytes 8 | tf_op jit(solution)/shard_map/psum | solution.py:42
  418.6 1.0 multiply_subtract_fusion.1
  419.6 3.3 multiply_reduce_fusion.1
  423.7 36.1 %psum.69 = f32[]{:T(128)} all-reduce(f32[]{:T(128)} %multiply_reduce_fusion.7), channel_id=1, replica_groups=mesh['cam'=16,'pts'=8] {'cam'}, use_global_device_ids=true, to_apply=%region_20.22 | all-reduce | flops 1 | bytes 8 | tf_op jit(solution)/shard_map/psum | solution.py:42
  461.0 0.8 fusion.35
  461.8 1.9 add.57
  463.7 1.0 copy.60
  464.8 1.0 copy.61
  465.8 1.2 gather_fusion.2
  467.3 9.1 %fusion.3 = bf16[64,1,192,1]{2,1,3,0:T(2,128)(2,1)S(1)} fusion(bf16[64,144,4,192]{3,2,1,0:T(4,128)(2,1)} %reshape.204, bf16[64,4,144,1]{2,1,0,3:T(4,128)(2,1)S(1)} %multiply_bitcast_fusion), kind=kOutput, calls=%fused_computation.9 | convolution fusion | flops 14155776 | bytes 14254080 | tf_op jit(solution)/shard_map/tckp,tkc->tp/dot_general | solution.py:54
  476.7 23.1 %all_gather.14 = bf16[16,3,4096]{2,1,0:T(4,128)(2,1)S(1)} all-gather(bf16[1,3,4096]{2,1,0:T(4,128)(2,1)S(1)} %convert_element_type.217), channel_id=1, replica_groups=mesh['cam'=16,'pts'=8] {'cam'}, dimensions={0}, use_global_device_ids=true | all-gather | bytes 417792 | tf_op jit(solution)/shard_map/all_gather | solution.py:58
  500.5 16.4 %fusion.2 = f32[64,144,4]{2,1,0:T(8,128)} fusion(f32[64,192]{1,0:T(8,128)S(1)} %copy.90, bf16[64,144,4,192]{3,2,1,0:T(4,128)(2,1)} %reshape.204), kind=kLoop, calls=%fused_computation.8 | loop fusion | flops 21196800 | bytes 14352384
  516.9 4.1 copy.87
  521.2 0.7 fusion.11
  522.5 2.5 convert_element_type.223
  525.0 3.3 multiply_reduce_fusion
  528.3 53.1 %all-reduce.9.cloned.1.call-done = bf16[9,8192]{1,0:T(8,128)(2,1)} async-done(((bf16[9,8192]{1,0:T(8,128)(2,1)}), bf16[9,8192]{1,0:T(8,128)(2,1)}) %all-reduce.9.cloned.1.call-update) | async-done | bytes 147472 | tf_op jit(solution)/shard_map/psum | solution.py:71
  581.4 1.7 multiply_reduce_fusion.6
  583.1 40.9 %psum.71 = f32[]{:T(128)} all-reduce(f32[]{:T(128)} %multiply_reduce_fusion.6), channel_id=1, replica_groups=mesh['cam'=16,'pts'=8] {'cam'}, use_global_device_ids=true, to_apply=%region_26.28 | all-reduce | flops 1 | bytes 8 | tf_op jit(solution)/shard_map/psum | solution.py:42
  625.4 2.1 multiply_subtract_fusion
  (75 shorter events, 9.9 us)
Async XLA Ops:
  7.2 163.4 %all-reduce.5.cloned.1.call-start = ((), (), s32[]{:S(2)}) async-start(), calls=%async_computation | async-start | bytes 524288 | tf_op jit(solution)/shard_map/psum | solution.py:71
  8.1 6.4 %copy-start.2 = (s32[64,1]{0,1:T(1,128)S(1)}, s32[64,1]{0,1:T(1,128)}, u32[]{:S(2)}) copy-start(s32[64,1]{0,1:T(1,128)} %param.15) | copy-start | bytes 772
  50.6 34.4 %copy-start.1 = (f32[3,3,4096]{2,1,0:T(4,128)S(1)}, f32[3,3,4096]{2,1,0:T(4,128)}, u32[]{:S(2)}) copy-start(f32[3,3,4096]{2,1,0:T(4,128)} %param.12) | copy-start | bytes 442372
  106.2 64.4 %copy-start = (f32[9,8192]{1,0:T(8,128)S(1)}, f32[9,8192]{1,0:T(8,128)}, u32[]{:S(2)}) copy-start(f32[9,8192]{1,0:T(8,128)} %param.9) | copy-start | bytes 884740
  110.1 264.4 %all-reduce.7.cloned.1.call-start = ((), (), s32[]{:S(2)}) async-start(), calls=%async_computation.1 | async-start | bytes 524288 | tf_op jit(solution)/shard_map/psum | solution.py:71
  318.1 263.3 %all-reduce.9.cloned.1.call-start = ((), (), s32[]{:S(2)}) async-start(), calls=%async_computation.2 | async-start | bytes 524288 | tf_op jit(solution)/shard_map/psum | solution.py:71
Sparse Core Ops, SparseCore 0:
  110.2 60.2 all-reduce.4
  318.2 56.2 all-reduce.6
  525.2 56.2 all-reduce.8
